TPU v7x, 32 devices: a whole 2x2x4 slice. The times are simulated.
32 devices in a mesh: groups: 2 (over x), ctx: 16 (over z, y, core).
Axes of the slice: x: 2, y: 2, z: 4, core: 2. Of those that a mesh axis runs over, the one named last changes fastest.
Arguments:
- queries: bfloat16 [2048, 4096], P(('groups', 'ctx')), parts along dimension 0, may hold values from -256 to 256
- text_keys: bfloat16 [2048, 512], P(('groups', 'ctx')), parts along dimension 0, may hold values from -4 to 4
- text_values: bfloat16 [2048, 512], P(('groups', 'ctx')), parts along dimension 0, may hold values from -5 to 5
- image_features: bfloat16 [16384, 256], P(('groups', 'ctx')), parts along dimension 0, may hold values from -300 to 300
- kv_weight: bfloat16 [8192, 1024], P('ctx'), may hold values from -0.0625 to 0.0625
- image_grids: int32 [32, 3], P(('groups', 'ctx')), parts along dimension 0, may hold values from 0 to 58, as said below
Outputs:
- attention: bfloat16 [2048, 4096], P(('groups', 'ctx')), parts along dimension 0
- cache_keys: bfloat16 [2048, 512], P(('groups', 'ctx')), parts along dimension 0
- cache_values: bfloat16 [2048, 512], P(('groups', 'ctx')), parts along dimension 0
There are 2 independent parts, one for each index of `groups`. A program takes and returns all parts, laid end to end along the dimension named above; an argument that names none is the same for every part. Nothing has to cross between parts.
Inputs may be any that keep to these rules, and one draw needn't show every extreme that they name: `image_grids`: row b describes the one image of context shard b: offset o, grid rows gh and grid columns gw with 2 <= gh, gw <= 4; its tokens take positions b * 64 + o to b * 64 + o + gh * gw - 1, token k at grid row k // gw and column k % gw; o + gh * gw <= 62; some shard has a 4 x 4 image.
All inputs are finite; a program needn't handle non-finite values.
Results may differ from a plain program's by a relative error of at most 0.0053.
Values may be sent and summed in bfloat16 or wider, within the bound.
No kernel may reach another device: no remote copies, remote signals or barrier semaphores. Data moves between devices by JAX's collectives and lax.ppermute only.
A program may use at most 128 MiB of HBM per device.

v0:
```python
import math
import jax
import jax.numpy as jnp
from jax import lax
from jax.sharding import PartitionSpec as P

D = 8192
HEAD_DIM = 128
GRID = 4


def rope_tables(time_ids, height_ids, width_ids):
    half_dim = HEAD_DIM // 2
    first_bound = HEAD_DIM // 8
    second_bound = first_bound + 3 * HEAD_DIM // 16
    pair_index = jnp.arange(half_dim, dtype=jnp.int32)
    inv_freq = 1000000.0 ** (-(2.0 * pair_index.astype(jnp.float32)) / HEAD_DIM)
    chosen = jnp.where(
        pair_index[None, :] < first_bound,
        time_ids[:, None],
        jnp.where(pair_index[None, :] < second_bound, height_ids[:, None], width_ids[:, None]),
    )
    angles = chosen.astype(jnp.float32) * inv_freq[None, :]
    cosine = jnp.concatenate([jnp.cos(angles), jnp.cos(angles)], axis=1)
    sine_table = jnp.concatenate([jnp.sin(angles), jnp.sin(angles)], axis=1)
    return (cosine, sine_table)


def rotate(key_heads, cosine, sine_table):
    half_dim = HEAD_DIM // 2
    turned = jnp.concatenate([-key_heads[..., half_dim:], key_heads[..., :half_dim]], axis=-1)
    return key_heads * cosine[:, None, :] + turned * sine_table[:, None, :]


def prepare(query_rows, kv_count, head_group):
    count_rows = query_rows.shape[0]
    shaped = query_rows.reshape(count_rows, kv_count, head_group, HEAD_DIM)
    return shaped.transpose(1, 2, 0, 3).reshape(kv_count, head_group * count_rows, HEAD_DIM)


def finish(summed, totals, count_rows, kv_count, head_group):
    blended = summed / totals[..., None]
    blended = blended.reshape(kv_count, head_group, count_rows, HEAD_DIM).transpose(2, 0, 1, 3)
    return blended.reshape(count_rows, kv_count * head_group * HEAD_DIM).astype(jnp.bfloat16)


def update(carry_state, query_set, positions, block_keys, block_values, key_start):
    running_max, running_sum, running_out = carry_state
    score_scale = 1.0 / math.sqrt(HEAD_DIM)
    scores = (
        jnp.einsum("grd,kgd->grk", query_set, block_keys, preferred_element_type=jnp.float32)
        * score_scale
    )
    key_pos = key_start + jnp.arange(block_keys.shape[0], dtype=jnp.int32)
    allowed = key_pos[None, None, :] <= positions[None, :, None]
    scores = jnp.where(allowed, scores, -1e30)
    new_max = jnp.maximum(running_max, jnp.max(scores, axis=-1))
    shrink = jnp.exp(running_max - new_max)
    weight = jnp.where(allowed, jnp.exp(scores - new_max[..., None]), 0.0)
    running_sum = running_sum * shrink + jnp.sum(weight, axis=-1)
    running_out = running_out * shrink[..., None] + jnp.einsum(
        "grk,kgd->grd",
        weight.astype(jnp.bfloat16),
        block_values,
        preferred_element_type=jnp.float32,
    )
    return (new_max, running_sum, running_out)


def body(queries, text_keys, text_values, image_features, kv_weight, image_grids):
    ctx_index = lax.axis_index("ctx")
    row_count = queries.shape[0]
    kv_width = text_keys.shape[1]
    kv_count = kv_width // HEAD_DIM
    head_group = queries.shape[1] // kv_width
    slot_count = GRID * GRID
    partial_kv = lax.dot_general(
        image_features, kv_weight, (((0,), (0,)), ((), ())), preferred_element_type=jnp.float32
    )
    feature_f32 = image_features.astype(jnp.float32)
    square_sums = jnp.sum(feature_f32 * feature_f32, axis=0)
    raw_kv, power_total = (
        lax.psum_scatter(partial_kv, "ctx", scatter_dimension=0, tiled=True),
        lax.psum_scatter(square_sums, "ctx", scatter_dimension=0, tiled=True),
    )
    normed = raw_kv * lax.rsqrt(power_total / D + 1e-06)[:, None]
    offset = image_grids[0, 0]
    grid_tall = image_grids[0, 1]
    grid_wide = image_grids[0, 2]
    within = jnp.arange(slot_count, dtype=jnp.int32)
    image_start = ctx_index * row_count + offset
    time_ids = jnp.broadcast_to(image_start, (slot_count,))
    height_ids = image_start + within // grid_wide
    width_ids = image_start + within % grid_wide
    cosine, sine_table = rope_tables(time_ids, height_ids, width_ids)
    key_heads = normed[:, :kv_width].reshape(slot_count, kv_count, HEAD_DIM)
    image_keys = (
        rotate(key_heads, cosine, sine_table).reshape(slot_count, kv_width).astype(jnp.bfloat16)
    )
    image_values = normed[:, kv_width:].astype(jnp.bfloat16)
    live_slot = within < grid_tall * grid_wide
    local_rows = jnp.arange(row_count, dtype=jnp.int32)
    one_hot = ((local_rows[:, None] == offset + within[None, :]) & live_slot[None, :]).astype(
        jnp.bfloat16
    )
    image_rows = (local_rows >= offset) & (local_rows < offset + grid_tall * grid_wide)
    placed = jnp.dot(
        one_hot,
        jnp.concatenate([image_keys, image_values], axis=1),
        preferred_element_type=jnp.float32,
    ).astype(jnp.bfloat16)
    cache_keys = jnp.where(image_rows[:, None], placed[:, :kv_width], text_keys)
    cache_values = jnp.where(image_rows[:, None], placed[:, kv_width:], text_values)
    half_rows = row_count // 2
    lead_queries = queries[:half_rows]
    trail_queries = queries[half_rows:]
    trail_base = ctx_index * row_count + half_rows
    lead_base = ctx_index * row_count
    query_sets = jnp.stack(
        [prepare(lead_queries, kv_count, head_group), prepare(trail_queries, kv_count, head_group)]
    )
    query_span = head_group * half_rows
    row_pos = jnp.arange(query_span, dtype=jnp.int32) % half_rows
    base_rows = jnp.stack([lead_base, trail_base])
    query_pos = base_rows[:, None] + row_pos[None, :]
    limits = base_rows + half_rows - 1
    initial = (
        jnp.full((2, kv_count, query_span), -1e30, jnp.float32),
        jnp.zeros((2, kv_count, query_span), jnp.float32),
        jnp.zeros((2, kv_count, query_span, HEAD_DIM), jnp.float32),
    )
    piece_keys = lax.all_gather(cache_keys, "ctx", axis=0, tiled=True)
    piece_values = lax.all_gather(cache_values, "ctx", axis=0, tiled=True)
    piece_size = piece_keys.shape[0]
    block_size = math.gcd(piece_size, 512)
    block_count = piece_size // block_size
    split_keys = piece_keys.reshape(block_count, block_size, kv_count, HEAD_DIM)
    split_values = piece_values.reshape(block_count, block_size, kv_count, HEAD_DIM)

    def scan_step(carried_state, scan_item):
        block_keys, block_values, number = scan_item
        key_start = number * block_size
        outcome = []
        for half_index in range(2):
            half_state = tuple((member[half_index] for member in carried_state))
            updated = lax.cond(
                key_start <= limits[half_index],
                lambda current: update(
                    current,
                    query_sets[half_index],
                    query_pos[half_index],
                    block_keys,
                    block_values,
                    key_start,
                ),
                lambda current: current,
                half_state,
            )
            outcome.append(updated)
        stacked = tuple(
            (
                jnp.stack([outcome[0][number_index], outcome[1][number_index]])
                for number_index in range(3)
            )
        )
        return (stacked, None)

    result_state, unused_out = lax.scan(
        scan_step, initial, (split_keys, split_values, jnp.arange(block_count, dtype=jnp.int32))
    )
    running_max, running_sum, running_out = result_state
    lead_out = finish(running_out[0], running_sum[0], half_rows, kv_count, head_group)
    trail_out = finish(running_out[1], running_sum[1], half_rows, kv_count, head_group)
    attention = jnp.concatenate([lead_out, trail_out], axis=0)
    return (attention, cache_keys, cache_values)


def solution(mesh):
    in_specs = (
        P(("groups", "ctx"), None),
        P(("groups", "ctx"), None),
        P(("groups", "ctx"), None),
        P(("groups", "ctx"), None),
        P("ctx", None),
        P(("groups", "ctx"), None),
    )
    out_specs = (P(("groups", "ctx"), None), P(("groups", "ctx"), None), P(("groups", "ctx"), None))
    return jax.shard_map(body, mesh=mesh, in_specs=in_specs, out_specs=out_specs, check_vma=False)
```

profile of v0, /device:TPU:25, one launch (start us, length us, event | category | flops | bytes accessed | tf_op | source)
XLA Modules:
  0.0 195.3 jit_solution(3191314341069254623)
XLA Ops:
  7.3 1.1 copy-done
  8.4 2.4 %fusion.47 = f32[256,1024]{1,0:T(8,128)} fusion(bf16[512,256]{1,0:T(8,128)(2,1)} %param.15, bf16[512,1024]{1,0:T(8,128)(2,1)S(1)} %copy-done), kind=kOutput, calls=%fused_computation.104 | convolution fusion | flops 268435456 | bytes 2359296 | tf_op jit(solution)/shard_map/dot_general | solution.py:77
  17.4 25.9 %all-reduce = f32[256]{0:T(256)S(1)} all-reduce(f32[256]{0:T(256)S(1)} %multiply_reduce_fusion), channel_id=3, replica_groups=mesh['groups'=2,'ctx'=16] {'ctx'}, use_global_device_ids=true, to_apply=%region_2.0.clone | all-reduce | flops 256 | bytes 2048
  45.8 21.6 %reduce-scatter.2.cloned.1.call-done = f32[16,1024]{1,0:T(8,128)} async-done(((f32[256,1024]{1,0:T(8,128)}), f32[16,1024]{1,0:T(8,128)}) %reduce-scatter.2.cloned.1.call-update) | async-done | bytes 65552 | tf_op jit(solution)/shard_map/reduce_scatter | solution.py:83
  67.4 0.9 broadcast_multiply_fusion
  70.5 0.8 copy.26
  71.4 37.9 %all-gather.3.cloned.1.call-done = bf16[1024,512]{1,0:T(8,128)(2,1)} async-done(((bf16[64,512]{1,0:T(8,128)(2,1)}), bf16[1024,512]{1,0:T(8,128)(2,1)}) %all-gather.3.cloned.1.call-update) | async-done | bytes 1048592 | tf_op jit(solution)/shard_map/all_gather | solution.py:132
  109.3 2.2 %reshape.193 = bf16[2,512,4,128]{3,2,1,0:T(4,128)(2,1)} reshape(bf16[1024,512]{1,0:T(8,128)(2,1)} %all-gather.3.cloned.1.call-done) | data formatting | bytes 2097152 | tf_op jit(solution)/shard_map/reshape | solution.py:137
  111.4 37.4 %all-gather.5.cloned.1.call-done = bf16[1024,512]{1,0:T(8,128)(2,1)} async-done(((bf16[64,512]{1,0:T(8,128)(2,1)}), bf16[1024,512]{1,0:T(8,128)(2,1)}) %all-gather.5.cloned.1.call-update) | async-done | bytes 1048592 | tf_op jit(solution)/shard_map/all_gather | solution.py:133
  148.9 2.1 %reshape.194 = bf16[2,512,4,128]{3,2,1,0:T(4,128)(2,1)} reshape(bf16[1024,512]{1,0:T(8,128)(2,1)} %all-gather.5.cloned.1.call-done) | data formatting | bytes 2097152 | tf_op jit(solution)/shard_map/reshape | solution.py:138
  151.1 35.4 %while.15 = (s32[]{:T(128)}, f32[2,4,256]{2,1,0:T(4,128)S(1)}, f32[2,4,256]{2,1,0:T(4,128)S(1)}, f32[2,4,256,128]{3,2,1,0:T(8,128)S(1)}, s32[2]{0:T(128)S(1)}, /...) while((s32[]{:T(128)}, f32[2,4,256]{2,1,0:T(4,128)S(1)}, ...), condition=%wide.region_12.13_spmd.clone, body=%wide.region_3.12_spmd.clone.sunk | while | flops 551560704 | bytes 36390424 | solution.py:168
  156.5 5.1 %conditional.6 = (f32[1,4,256]{2,1,0:T(4,128)}, f32[1,4,256]{2,1,0:T(4,128)S(1)}, f32[1,4,256,128]{3,2,1,0:T(8,128)S(1)}) conditional(s32[]{:T(128)} %convert_element_type.81, (f32[4,256]{1,0:T(4,128)}, f32[4,256]{1,0:T(4,128)S(1)}, f32[4,256,128]{2,1,0:T(8,128)S(1)}) %tuple.139, (s32[]{:T(128)}, s32[2,256]{1,0:T(2,128)S(1)}, ...), branch_computations={%region_8.8_spmd, %region_9.11_spmd} | conditional | flops 275646976 | bytes 9239580 | solution.py:146
  157.8 1.5 fusion.16
  160.0 1.6 fusion.17
  162.9 5.1 %conditional.7 = (f32[1,4,256]{2,1,0:T(4,128)}, f32[1,4,256]{2,1,0:T(4,128)S(1)}, f32[1,4,256,128]{3,2,1,0:T(8,128)S(1)}) conditional(s32[]{:T(128)} %convert_element_type.82, (f32[4,256]{1,0:T(4,128)}, f32[4,256]{1,0:T(4,128)S(1)}, f32[4,256,128]{2,1,0:T(8,128)S(1)}) %tuple.141, (s32[]{:T(128)}, s32[2,256]{1,0:T(2,128)S(1)}, ...), branch_computations={%region_4.4_spmd, %region_5.7_spmd} | conditional | flops 275646976 | bytes 9239580 | solution.py:146
  164.3 1.5 fusion.4
  166.4 1.6 fusion.5
  174.2 5.1 %conditional.6 = (f32[1,4,256]{2,1,0:T(4,128)}, f32[1,4,256]{2,1,0:T(4,128)S(1)}, f32[1,4,256,128]{3,2,1,0:T(8,128)S(1)}) conditional(s32[]{:T(128)} %convert_element_type.81, (f32[4,256]{1,0:T(4,128)}, f32[4,256]{1,0:T(4,128)S(1)}, f32[4,256,128]{2,1,0:T(8,128)S(1)}) %tuple.139, (s32[]{:T(128)}, s32[2,256]{1,0:T(2,128)S(1)}, ...), branch_computations={%region_8.8_spmd, %region_9.11_spmd} | conditional | flops 275646976 | bytes 9239580 | solution.py:146
  175.5 1.5 fusion.16
  177.7 1.6 fusion.17
  180.6 5.1 %conditional.7 = (f32[1,4,256]{2,1,0:T(4,128)}, f32[1,4,256]{2,1,0:T(4,128)S(1)}, f32[1,4,256,128]{3,2,1,0:T(8,128)S(1)}) conditional(s32[]{:T(128)} %convert_element_type.82, (f32[4,256]{1,0:T(4,128)}, f32[4,256]{1,0:T(4,128)S(1)}, f32[4,256,128]{2,1,0:T(8,128)S(1)}) %tuple.141, (s32[]{:T(128)}, s32[2,256]{1,0:T(2,128)S(1)}, ...), branch_computations={%region_4.4_spmd, %region_5.7_spmd} | conditional | flops 275646976 | bytes 9239580 | solution.py:146
  182.0 1.5 fusion.4
  184.1 1.6 fusion.5
  187.9 0.8 pad_maximum_fusion.3
  (123 shorter events, 26.3 us)
Async XLA Ops:
  7.2 1.2 copy-start
  7.2 8.9 %copy-start.9 = (u32[32]{0:T(128)S(1)}, u32[32]{0:T(128)}, u32[]{:S(2)}) copy-start(u32[32]{0:T(128)} %constant.92) | copy-start | bytes 388
  7.2 10.1 %copy-start.4 = (bf16[512,256]{1,0:T(8,128)(2,1)S(1)}, bf16[512,256]{1,0:T(8,128)(2,1)}, u32[]{:S(2)}) copy-start(bf16[512,256]{1,0:T(8,128)(2,1)} %param.15) | copy-start | bytes 786436
  7.2 3.7 %copy-start.8 = (s32[1,3]{1,0:T(1,128)S(1)}, s32[1,3]{1,0:T(1,128)}, u32[]{:S(2)}) copy-start(s32[1,3]{1,0:T(1,128)} %param.17) | copy-start | bytes 40
  7.2 61.5 %copy-start.6 = (bf16[64,512]{1,0:T(8,128)(2,1)S(1)}, bf16[64,512]{1,0:T(8,128)(2,1)}, u32[]{:S(2)}) copy-start(bf16[64,512]{1,0:T(8,128)(2,1)} %param.14) | copy-start | bytes 196612
  7.2 61.5 %copy-start.7 = (bf16[64,512]{1,0:T(8,128)(2,1)S(1)}, bf16[64,512]{1,0:T(8,128)(2,1)}, u32[]{:S(2)}) copy-start(bf16[64,512]{1,0:T(8,128)(2,1)} %param.13) | copy-start | bytes 196612
  7.2 63.0 %copy-start.5 = (bf16[64,4096]{1,0:T(8,128)(2,1)S(1)}, bf16[64,4096]{1,0:T(8,128)(2,1)}, u32[]{:S(2)}) copy-start(bf16[64,4096]{1,0:T(8,128)(2,1)} %param.12) | copy-start | bytes 1572868
  7.2 60.1 %reduce-scatter.2.cloned.1.call-start = ((), (), s32[]{:S(2)}) async-start(), calls=%async_computation.1 | async-start | bytes 1114112 | tf_op jit(solution)/shard_map/reduce_scatter | solution.py:83
  10.8 98.4 %all-gather.3.cloned.1.call-start = ((), (), s32[]{:S(2)}) async-start(), calls=%async_computation.2 | async-start | bytes 1114112 | tf_op jit(solution)/shard_map/all_gather | solution.py:132
  69.5 79.4 %all-gather.5.cloned.1.call-start = ((), (), s32[]{:S(2)}) async-start(), calls=%async_computation.3 | async-start | bytes 1114112 | tf_op jit(solution)/shard_map/all_gather | solution.py:133
  153.7 1.2 copy-start.1
  153.8 1.5 copy-start.2
  155.3 1.2 copy-start.3
  171.4 1.2 copy-start.1
  171.4 1.5 copy-start.2
  173.0 1.2 copy-start.3
Sparse Core Ops, SparseCore 0:
  11.7 55.6 reduce-scatter.1
  70.1 39.1 all-gather.2
  112.0 36.8 all-gather.4
where the time goes:
time: 196 us; the launch traced here: 195 us
  waiting for transfers between devices  97.6 us (50%)
  blocking collectives  25.9 us (13%)
  other arithmetic  19.3 us (10%)
  between operations  19.2 us (10%)
  local copies, waits for them, and re-layouts  17.6 us (9%)
  matrix products  11.3 us (6%)
  loops' own time  4.18 us (2%)
    all_gather x1, waiting for transfers between devices, body(): piece_keys = lax.all_gather(cache_keys, 'ctx', axis=0, tiled=True)  37.9 us
    all_gather x1, waiting for transfers between devices, body(): piece_values = lax.all_gather(cache_values, 'ctx', axis=0, tiled=True)  37.4 us
    unnamed x1, blocking collectives  25.9 us
    reduce_scatter x1, waiting for transfers between devices, body(): lax.psum_scatter(partial_kv, 'ctx', scatter_dimension=0, tiled=True)  21.6 us
    dot_general x4, matrix products, update(): jnp.einsum('grk,kgd->grd', weight.astype(jnp.bfloat16), block_values, pre...  6.43 us
    reduce_sum x4, other arithmetic, update(): running_sum = running_sum * shrink + jnp.sum(weight, axis=-1)  5.93 us
    while x16, local copies, waits for them, and re-layouts  4.29 us
    another operation x10, other arithmetic, scan_step(): jnp.stack([outcome[0][number_index], outcome[1][number_index]])  4.27 us
  transfers between devices with their start and end apart: 3, of which 3 were waited for; matrix products, arithmetic and copies ran while one was open for 4% of the time, Pallas kernels for 0%

commit v1 on v0

--- a/solution.py
+++ b/solution.py
@@ -129,7 +129,15 @@
         jnp.zeros((2, kv_count, query_span), jnp.float32),
         jnp.zeros((2, kv_count, query_span, HEAD_DIM), jnp.float32),
     )
-    piece_keys = lax.all_gather(cache_keys, "ctx", axis=0, tiled=True)
+    ways, here = (lax.axis_size("ctx"), lax.axis_index("ctx"))
+    grown, reach = (cache_keys, 1)
+    while reach < ways:
+        theirs = lax.ppermute(grown, "ctx", [(d, d ^ reach) for d in range(ways)])
+        mine_first = jnp.concatenate([grown, theirs], axis=0)
+        theirs_first = jnp.concatenate([theirs, grown], axis=0)
+        grown = jnp.where(here & reach == 0, mine_first, theirs_first)
+        reach = 2 * reach
+    piece_keys = grown
     piece_values = lax.all_gather(cache_values, "ctx", axis=0, tiled=True)
     piece_size = piece_keys.shape[0]
     block_size = math.gcd(piece_size, 512)

time: 196 us -> 171 us (0.87)
  waiting for transfers between devices: 97.6 us -> 65.4 us
  starting transfers between devices: 0.12 us -> 5.66 us
    all_gather x1 -> x0, waiting for transfers between devices: 37.9 us -> none  [body(): piece_keys = lax.all_gather(cache_keys, 'ctx', axis=0, tiled=True)]
    ppermute x0 -> x4, waiting for transfers between devices: none -> 36.5 us  [body(): theirs = lax.ppermute(grown, 'ctx', [(d, d ^ reach) for d in range(ways)])]
    all_gather x1, waiting for transfers between devices: 37.4 us -> 7.25 us  [body(): piece_values = lax.all_gather(cache_values, 'ctx', axis=0, tiled=True)]
    ppermute x0 -> x4, starting transfers between devices: none -> 5.58 us  [body(): theirs = lax.ppermute(grown, 'ctx', [(d, d ^ reach) for d in range(ways)])]
    reshape x1 -> x0, local copies, waits for them, and re-layouts: 2.16 us -> none  [body(): split_keys = piece_keys.reshape(block_count, block_size, kv_count, HEAD_DIM)]
  transfers between devices with their start and end apart: 3 -> 6, of which waited for: 3 -> 6; matrix products, arithmetic and copies ran while one was open for 4% -> 5% of each run, Pallas kernels for 0% -> 0%
where the time goes in v1:
time: 171 us; the launch traced here: 170 us
  waiting for transfers between devices  65.4 us (38%)
  blocking collectives  25.9 us (15%)
  other arithmetic  20.1 us (12%)
  between operations  19.5 us (11%)
  local copies, waits for them, and re-layouts  17.6 us (10%)
  matrix products  11.4 us (7%)
  starting transfers between devices  5.66 us (3%)
  loops' own time  4.21 us (2%)
    ppermute x4, waiting for transfers between devices, body(): theirs = lax.ppermute(grown, 'ctx', [(d, d ^ reach) for d in range(ways)])  36.5 us
    unnamed x1, blocking collectives  25.9 us
    reduce_scatter x1, waiting for transfers between devices, body(): lax.psum_scatter(partial_kv, 'ctx', scatter_dimension=0, tiled=True)  21.6 us
    all_gather x1, waiting for transfers between devices, body(): piece_values = lax.all_gather(cache_values, 'ctx', axis=0, tiled=True)  7.25 us
    dot_general x4, matrix products, update(): jnp.einsum('grk,kgd->grd', weight.astype(jnp.bfloat16), block_values, pre...  6.52 us
    reduce_sum x4, other arithmetic, update(): running_sum = running_sum * shrink + jnp.sum(weight, axis=-1)  5.94 us
    ppermute x4, starting transfers between devices, body(): theirs = lax.ppermute(grown, 'ctx', [(d, d ^ reach) for d in range(ways)])  5.58 us
    another operation x10, other arithmetic, scan_step(): jnp.stack([outcome[0][number_index], outcome[1][number_index]])  4.29 us
  transfers between devices with their start and end apart: 6, of which 6 were waited for; matrix products, arithmetic and copies ran while one was open for 5% of the time, Pallas kernels for 0%

profile of v1, /device:TPU:25, one launch (start us, length us, event | category | flops | bytes accessed | tf_op | source)
XLA Modules:
  0.0 169.7 jit_solution(17624262522089523670)
XLA Ops:
  8.4 2.4 %fusion.47 = f32[256,1024]{1,0:T(8,128)} fusion(bf16[512,256]{1,0:T(8,128)(2,1)} %param.15, bf16[512,1024]{1,0:T(8,128)(2,1)S(1)} %copy-done), kind=kOutput, calls=%fused_computation.108 | convolution fusion | flops 268435456 | bytes 2359296 | tf_op jit(solution)/shard_map/dot_general | solution.py:77
  17.4 25.9 %all-reduce = f32[256]{0:T(256)S(1)} all-reduce(f32[256]{0:T(256)S(1)} %multiply_reduce_fusion), channel_id=3, replica_groups=mesh['groups'=2,'ctx'=16] {'ctx'}, use_global_device_ids=true, to_apply=%region_2.0.clone | all-reduce | flops 256 | bytes 2048
  45.8 21.6 %reduce-scatter.2.cloned.1.call-done = f32[16,1024]{1,0:T(8,128)} async-done(((f32[256,1024]{1,0:T(8,128)}), f32[16,1024]{1,0:T(8,128)}) %reduce-scatter.2.cloned.1.call-update) | async-done | bytes 65552 | tf_op jit(solution)/shard_map/reduce_scatter | solution.py:83
  69.4 2.7 %collective-permute-start = (bf16[64,512]{1,0:T(8,128)(2,1)S(1)}, bf16[64,512]{1,0:T(8,128)(2,1)S(1)}, u32[]{:S(2)}, u32[]{:S(2)}) collective-permute-start(bf16[64,512]{1,0:T(8,128)(2,1)S(1)} %get-tuple-element.298), channel_id=1, source_target_pairs={{0,1},{1,0},{2,3},{3,2},{4,5},{5,4},{6,7},{7,6},{8,9},{9,8},{10,11... | collective-permute-start | bytes 196616 | tf_op jit(solution)/shard_map/ppermute | solution.py:135
  73.4 4.4 %collective-permute-done.1 = bf16[128,512]{1,0:T(8,128)(2,1)S(1)} collective-permute-done((bf16[128,512]{1,0:T(8,128)(2,1)S(1)}, bf16[128,512]{1,0:T(8,128)(2,1)S(1)}, u32[]{:S(2)}, u32[]{:S(2)}) %collective-permute-start.1) | collective-permute-done | bytes 131104 | tf_op jit(solution)/shard_map/ppermute | solution.py:135
  78.2 7.5 %collective-permute-done.2 = bf16[256,512]{1,0:T(8,128)(2,1)S(1)} collective-permute-done((bf16[256,512]{1,0:T(8,128)(2,1)S(1)}, bf16[256,512]{1,0:T(8,128)(2,1)S(1)}, u32[]{:S(2)}, u32[]{:S(2)}) %collective-permute-start.2) | collective-permute-done | bytes 262176 | tf_op jit(solution)/shard_map/ppermute | solution.py:135
  86.0 2.2 %collective-permute-start.3 = (bf16[512,512]{1,0:T(8,128)(2,1)S(1)}, bf16[512,512]{1,0:T(8,128)(2,1)S(1)}, u32[]{:S(2)}, u32[]{:S(2)}) collective-permute-start(bf16[512,512]{1,0:T(8,128)(2,1)S(1)} %maximum_select_fusion.1), channel_id=1, source_target_pairs={{0,8},{1,9},{2,10},{3,11},{4,12},{5,13},{6,14},{7,15},{8,0},{9,1},... | collective-permute-start | bytes 1572872 | tf_op jit(solution)/shard_map/ppermute | solution.py:135
  90.3 23.7 %collective-permute-done.3 = bf16[512,512]{1,0:T(8,128)(2,1)S(1)} collective-permute-done((bf16[512,512]{1,0:T(8,128)(2,1)S(1)}, bf16[512,512]{1,0:T(8,128)(2,1)S(1)}, u32[]{:S(2)}, u32[]{:S(2)}) %collective-permute-start.3) | collective-permute-done | bytes 524320 | tf_op jit(solution)/shard_map/ppermute | solution.py:135
  114.5 1.1 select_n.110
  115.6 7.3 %all-gather.2.cloned.1.call-done = bf16[1024,512]{1,0:T(8,128)(2,1)} async-done(((bf16[64,512]{1,0:T(8,128)(2,1)}), bf16[1024,512]{1,0:T(8,128)(2,1)}) %all-gather.2.cloned.1.call-update) | async-done | bytes 1048592 | tf_op jit(solution)/shard_map/all_gather | solution.py:141
  122.9 2.1 %reshape.195 = bf16[2,512,4,128]{3,2,1,0:T(4,128)(2,1)} reshape(bf16[1024,512]{1,0:T(8,128)(2,1)} %all-gather.2.cloned.1.call-done) | data formatting | bytes 2097152 | tf_op jit(solution)/shard_map/reshape | solution.py:146
  125.1 35.5 %while.15 = (s32[]{:T(128)}, f32[2,4,256]{2,1,0:T(4,128)S(1)}, f32[2,4,256]{2,1,0:T(4,128)S(1)}, f32[2,4,256,128]{3,2,1,0:T(8,128)S(1)}, s32[2]{0:T(128)S(1)}, /...) while((s32[]{:T(128)}, f32[2,4,256]{2,1,0:T(4,128)S(1)}, ...), condition=%wide.region_12.13_spmd.clone, body=%wide.region_3.12_spmd.clone.sunk | while | flops 551560704 | bytes 36390424 | solution.py:176
  130.4 5.1 %conditional.6 = (f32[1,4,256]{2,1,0:T(4,128)}, f32[1,4,256]{2,1,0:T(4,128)S(1)}, f32[1,4,256,128]{3,2,1,0:T(8,128)S(1)}) conditional(s32[]{:T(128)} %convert_element_type.81, (f32[4,256]{1,0:T(4,128)}, f32[4,256]{1,0:T(4,128)S(1)}, f32[4,256,128]{2,1,0:T(8,128)S(1)}) %tuple.139, (s32[]{:T(128)}, s32[2,256]{1,0:T(2,128)S(1)}, ...), branch_computations={%region_8.8_spmd, %region_9.11_spmd} | conditional | flops 275646976 | bytes 9239580 | solution.py:154
  131.8 1.5 fusion.16
  134.0 1.6 fusion.17
  136.9 5.2 %conditional.7 = (f32[1,4,256]{2,1,0:T(4,128)}, f32[1,4,256]{2,1,0:T(4,128)S(1)}, f32[1,4,256,128]{3,2,1,0:T(8,128)S(1)}) conditional(s32[]{:T(128)} %convert_element_type.82, (f32[4,256]{1,0:T(4,128)}, f32[4,256]{1,0:T(4,128)S(1)}, f32[4,256,128]{2,1,0:T(8,128)S(1)}) %tuple.141, (s32[]{:T(128)}, s32[2,256]{1,0:T(2,128)S(1)}, ...), branch_computations={%region_4.4_spmd, %region_5.7_spmd} | conditional | flops 275646976 | bytes 9239580 | solution.py:154
  138.2 1.5 fusion.4
  140.4 1.6 fusion.5
  148.2 5.1 %conditional.6 = (f32[1,4,256]{2,1,0:T(4,128)}, f32[1,4,256]{2,1,0:T(4,128)S(1)}, f32[1,4,256,128]{3,2,1,0:T(8,128)S(1)}) conditional(s32[]{:T(128)} %convert_element_type.81, (f32[4,256]{1,0:T(4,128)}, f32[4,256]{1,0:T(4,128)S(1)}, f32[4,256,128]{2,1,0:T(8,128)S(1)}) %tuple.139, (s32[]{:T(128)}, s32[2,256]{1,0:T(2,128)S(1)}, ...), branch_computations={%region_8.8_spmd, %region_9.11_spmd} | conditional | flops 275646976 | bytes 9239580 | solution.py:154
  149.6 1.5 fusion.16
  151.7 1.6 fusion.17
  154.7 5.2 %conditional.7 = (f32[1,4,256]{2,1,0:T(4,128)}, f32[1,4,256]{2,1,0:T(4,128)S(1)}, f32[1,4,256,128]{3,2,1,0:T(8,128)S(1)}) conditional(s32[]{:T(128)} %convert_element_type.82, (f32[4,256]{1,0:T(4,128)}, f32[4,256]{1,0:T(4,128)S(1)}, f32[4,256,128]{2,1,0:T(8,128)S(1)}) %tuple.141, (s32[]{:T(128)}, s32[2,256]{1,0:T(2,128)S(1)}, ...), branch_computations={%region_4.4_spmd, %region_5.7_spmd} | conditional | flops 275646976 | bytes 9239580 | solution.py:154
  156.0 1.5 fusion.4
  158.2 1.6 fusion.5
  (132 shorter events, 32.6 us)
Async XLA Ops:
  7.2 1.2 copy-start
  7.2 8.9 %copy-start.9 = (u32[32]{0:T(128)S(1)}, u32[32]{0:T(128)}, u32[]{:S(2)}) copy-start(u32[32]{0:T(128)} %constant.99) | copy-start | bytes 388
  7.2 10.1 %copy-start.4 = (bf16[512,256]{1,0:T(8,128)(2,1)S(1)}, bf16[512,256]{1,0:T(8,128)(2,1)}, u32[]{:S(2)}) copy-start(bf16[512,256]{1,0:T(8,128)(2,1)} %param.15) | copy-start | bytes 786436
  7.2 3.7 %copy-start.8 = (s32[1,3]{1,0:T(1,128)S(1)}, s32[1,3]{1,0:T(1,128)}, u32[]{:S(2)}) copy-start(s32[1,3]{1,0:T(1,128)} %param.17) | copy-start | bytes 40
  7.2 61.5 %copy-start.6 = (bf16[64,512]{1,0:T(8,128)(2,1)S(1)}, bf16[64,512]{1,0:T(8,128)(2,1)}, u32[]{:S(2)}) copy-start(bf16[64,512]{1,0:T(8,128)(2,1)} %param.14) | copy-start | bytes 196612
  7.2 61.5 %copy-start.7 = (bf16[64,512]{1,0:T(8,128)(2,1)S(1)}, bf16[64,512]{1,0:T(8,128)(2,1)}, u32[]{:S(2)}) copy-start(bf16[64,512]{1,0:T(8,128)(2,1)} %param.13) | copy-start | bytes 196612
  7.2 60.1 %reduce-scatter.2.cloned.1.call-start = ((), (), s32[]{:S(2)}) async-start(), calls=%async_computation.1 | async-start | bytes 1114112 | tf_op jit(solution)/shard_map/reduce_scatter | solution.py:83
  10.8 112.0 %all-gather.2.cloned.1.call-start = ((), (), s32[]{:S(2)}) async-start(), calls=%async_computation.2 | async-start | bytes 1114112 | tf_op jit(solution)/shard_map/all_gather | solution.py:141
  69.4 20.0 %copy-start.5 = (bf16[64,512]{1,0:T(8,128)(2,1)}, bf16[64,512]{1,0:T(8,128)(2,1)S(1)}, u32[]{:S(2)}) copy-start(bf16[64,512]{1,0:T(8,128)(2,1)S(1)} %get-tuple-element.298) | copy-start | bytes 196612
  69.4 3.6 %collective-permute-start = (bf16[64,512]{1,0:T(8,128)(2,1)S(1)}, bf16[64,512]{1,0:T(8,128)(2,1)S(1)}, u32[]{:S(2)}, u32[]{:S(2)}) collective-permute-start(bf16[64,512]{1,0:T(8,128)(2,1)S(1)} %get-tuple-element.298), channel_id=1, source_target_pairs={{0,1},{1,0},{2,3},{3,2},{4,5},{5,4},{6,7},{7,6},{8,9},{9,8},{10,11... | collective-permute-start | bytes 196616 | tf_op jit(solution)/shard_map/ppermute | solution.py:135
  73.1 4.8 %collective-permute-start.1 = (bf16[128,512]{1,0:T(8,128)(2,1)S(1)}, bf16[128,512]{1,0:T(8,128)(2,1)S(1)}, u32[]{:S(2)}, u32[]{:S(2)}) collective-permute-start(bf16[128,512]{1,0:T(8,128)(2,1)S(1)} %maximum_select_fusion.3), channel_id=1, source_target_pairs={{0,2},{1,3},{2,0},{3,1},{4,6},{5,7},{6,4},{7,5},{8,10},{9,11},{10,... | collective-permute-start | bytes 393224 | tf_op jit(solution)/shard_map/ppermute | solution.py:135
  77.9 7.9 %collective-permute-start.2 = (bf16[256,512]{1,0:T(8,128)(2,1)S(1)}, bf16[256,512]{1,0:T(8,128)(2,1)S(1)}, u32[]{:S(2)}, u32[]{:S(2)}) collective-permute-start(bf16[256,512]{1,0:T(8,128)(2,1)S(1)} %maximum_select_fusion.2), channel_id=1, source_target_pairs={{0,4},{1,5},{2,6},{3,7},{4,0},{5,1},{6,2},{7,3},{8,12},{9,13},{10,... | collective-permute-start | bytes 786440 | tf_op jit(solution)/shard_map/ppermute | solution.py:135
  86.0 28.1 %collective-permute-start.3 = (bf16[512,512]{1,0:T(8,128)(2,1)S(1)}, bf16[512,512]{1,0:T(8,128)(2,1)S(1)}, u32[]{:S(2)}, u32[]{:S(2)}) collective-permute-start(bf16[512,512]{1,0:T(8,128)(2,1)S(1)} %maximum_select_fusion.1), channel_id=1, source_target_pairs={{0,8},{1,9},{2,10},{3,11},{4,12},{5,13},{6,14},{7,15},{8,0},{9,1},... | collective-permute-start | bytes 1572872 | tf_op jit(solution)/shard_map/ppermute | solution.py:135
  127.7 1.2 copy-start.1
  127.7 1.5 copy-start.2
  129.2 1.2 copy-start.3
  145.5 1.2 copy-start.1
  145.5 1.5 copy-start.2
  147.0 1.2 copy-start.3
Sparse Core Ops, SparseCore 0:
  11.7 55.6 reduce-scatter.1
  70.1 52.7 all-gather.1
